TPU v7x, 32 devices: a whole 2x2x4 slice. The times are simulated.
32 devices in a mesh: box: 4 (over y, core), dir: 8 (over z, x).
Axes of the slice: x: 2, y: 2, z: 4, core: 2. Of those that a mesh axis runs over, the one named last changes fastest.
Arguments:
- currents: bfloat16 [256, 2, 256, 128], P(('box', 'dir')), may hold values from -6 to 6
- near_blocks: bfloat16 [256, 3, 2, 256, 256], P(('box', 'dir')), may hold values from -0.21875 to 0.21875
- near_mask: int32 [2, 256], replicated, may hold values 0 or 1
- aggregate: bfloat16 [2, 512, 256], replicated, may hold values from -0.375 to 0.375
- disaggregate: bfloat16 [2, 256, 512], replicated, may hold values from -0.25 to 0.25
- centers: float32 [3, 256], replicated, may hold values from 0 to 16
Outputs:
- fields: bfloat16 [256, 2, 256, 128], P(('box', 'dir'))
All inputs are finite; a program needn't handle non-finite values.
Results may differ from a plain program's by a relative error of at most 0.0054.
Values may be sent and summed in bfloat16 or wider, within the bound.
No kernel may reach another device: no remote copies, remote signals or barrier semaphores. Data moves between devices by JAX's collectives and lax.ppermute only.
A program may use at most 64 MiB of HBM per device.

v0:
```python
import math
import jax
import jax.numpy as jnp
from jax import lax
from jax.sharding import PartitionSpec as P

wave_number = 2.0
far_gain = 8.0
golden_turn = 2.399963229728653


def extended(block, sides, width):
    for axis, dim in sides:
        count = lax.axis_size(axis)
        forward = [(i, i + 1) for i in range(count - 1)]
        backward = [(target, source) for source, target in forward]
        low = lax.ppermute(
            lax.slice_in_dim(block, block.shape[dim] - width, None, axis=dim), axis, forward
        )
        high = lax.ppermute(lax.slice_in_dim(block, 0, width, axis=dim), axis, backward)
        block = jnp.concatenate([low, block, high], axis=dim)
    return block


def direction_cosines(count, first, many):
    order = (first + jnp.arange(many, dtype=jnp.int32)).astype(jnp.float32)
    height = 1.0 - (2.0 * order + 1.0) / count
    radial = jnp.sqrt(1.0 - height * height)
    azimuth = order * golden_turn
    return (radial * jnp.cos(azimuth), radial * jnp.sin(azimuth), height)


def phase_angles(points, first, many, count):
    dir_x, dir_y, dir_z = direction_cosines(count, first, many)
    return wave_number * (
        points[0][:, None] * dir_x[None, :]
        + points[1][:, None] * dir_y[None, :]
        + points[2][:, None] * dir_z[None, :]
    )


def far_matrix(centers, near_mask):
    total_boxes = centers.shape[1]
    squared = jnp.zeros((total_boxes, total_boxes), jnp.float32)
    for axis_number in range(3):
        spread = centers[axis_number][:, None] - centers[axis_number][None, :]
        squared = squared + spread * spread
    spacing = jnp.sqrt(1.0 + squared)
    kernel = jnp.cos(wave_number * spacing) / (1.0 + spacing) * (far_gain / math.sqrt(total_boxes))
    rows = jnp.arange(total_boxes, dtype=jnp.int32)[:, None]
    cols = jnp.arange(total_boxes, dtype=jnp.int32)[None, :]
    linked = (
        (cols == rows)
        | (cols == rows - 1) & (near_mask[0][:, None] == 1)
        | (cols == rows + 1) & (near_mask[1][:, None] == 1)
    )
    return jnp.where(linked, 0.0, kernel).astype(jnp.bfloat16)


def near_field(currents, near_blocks, own_mask):
    padded = extended(currents, ((("box", "dir"), 0),), 1)
    left_on = own_mask[0].astype(jnp.bfloat16)[:, None, None, None]
    right_on = own_mask[1].astype(jnp.bfloat16)[:, None, None, None]
    stacked = jnp.stack([currents, padded[:-2] * left_on, padded[2:] * right_on], 1)

    def product(left, right):
        return jnp.einsum("bjuv,bjva->bua", left, right, preferred_element_type=jnp.float32)

    block_re = near_blocks[:, :, 0]
    block_im = near_blocks[:, :, 1]
    near_re = product(block_re, stacked[:, :, 0]) - product(block_im, stacked[:, :, 1])
    near_im = product(block_re, stacked[:, :, 1]) + product(block_im, stacked[:, :, 0])
    return jnp.stack([near_re, near_im], 1)


def local(currents, near_blocks, near_mask, aggregate, disaggregate, centers):
    device_index = lax.axis_index(("box", "dir"))
    devices = lax.axis_size(("box", "dir"))
    box_count = currents.shape[0]
    total_boxes = centers.shape[1]
    dir_count = aggregate.shape[1]
    dir_share = dir_count // devices
    angle_count = currents.shape[3]
    own_centers = lax.dynamic_slice_in_dim(centers, device_index * box_count, box_count, 1)
    own_mask = lax.dynamic_slice_in_dim(near_mask, device_index * box_count, box_count, 1)
    near = near_field(currents, near_blocks, own_mask)

    def gather_in(matrix, vectors):
        return jnp.einsum("ku,bua->bka", matrix, vectors, preferred_element_type=jnp.float32)

    pat_re = gather_in(aggregate[0], currents[:, 0]) - gather_in(aggregate[1], currents[:, 1])
    pat_im = gather_in(aggregate[0], currents[:, 1]) + gather_in(aggregate[1], currents[:, 0])
    theta = phase_angles(own_centers, 0, dir_count, dir_count)
    cosine = jnp.cos(theta)[:, :, None]
    sine = jnp.sin(theta)[:, :, None]
    pattern = jnp.stack(
        [cosine * pat_re + sine * pat_im, cosine * pat_im - sine * pat_re], 2
    ).astype(jnp.bfloat16)
    arrived = lax.all_to_all(pattern[None], ("box", "dir"), split_axis=2, concat_axis=0, tiled=True)
    flat_pattern = arrived.reshape(total_boxes, dir_share * 2 * angle_count)
    translate = far_matrix(centers, near_mask)
    summed = jnp.dot(translate, flat_pattern, preferred_element_type=jnp.float32).reshape(
        total_boxes, dir_share, 2, angle_count
    )
    theta_all = phase_angles(centers, device_index * dir_share, dir_share, dir_count)
    cos_all = jnp.cos(theta_all)[:, :, None]
    sin_all = jnp.sin(theta_all)[:, :, None]
    sum_re = summed[:, :, 0]
    sum_im = summed[:, :, 1]
    received = jnp.stack(
        [cos_all * sum_re - sin_all * sum_im, cos_all * sum_im + sin_all * sum_re], 2
    ).astype(jnp.bfloat16)
    shaped_back = received.reshape(devices, box_count, dir_share, 2, angle_count)
    returned = lax.all_to_all(shaped_back, ("box", "dir"), split_axis=0, concat_axis=2, tiled=True)
    returned = returned.reshape(box_count, dir_count, 2, angle_count)

    def spread_out(matrix, vectors):
        return jnp.einsum("uk,bka->bua", matrix, vectors, preferred_element_type=jnp.float32)

    far_re = spread_out(disaggregate[0], returned[:, :, 0]) - spread_out(
        disaggregate[1], returned[:, :, 1]
    )
    far_im = spread_out(disaggregate[0], returned[:, :, 1]) + spread_out(
        disaggregate[1], returned[:, :, 0]
    )
    far = jnp.stack([far_re, far_im], 1)
    return (near + far).astype(jnp.bfloat16)


def solution(mesh):
    return jax.shard_map(
        local,
        mesh=mesh,
        in_specs=(
            P(("box", "dir"), None, None, None),
            P(("box", "dir"), None, None, None, None),
            P(),
            P(),
            P(),
            P(),
        ),
        out_specs=P(("box", "dir"), None, None, None),
        check_vma=False,
    )
```

profile of v0, /device:TPU:17, one launch (start us, length us, event | category | flops | bytes accessed | tf_op | source)
XLA Modules:
  0.0 152.9 jit_solution(14616655353102153419)
XLA Ops:
  0.0 0.0 copy-start
  0.1 1.5 %copy.35 = bf16[8,2,256,128]{2,3,0,1:T(8,128)(2,1)S(1)} copy(bf16[8,2,256,128]{3,2,1,0:T(8,128)(2,1)} %param.6) | data formatting | bytes 2097152 | tf_op args[0]
  1.6 0.0 copy-done
  1.6 0.0 copy-start.1
  1.6 1.8 %fusion.50 = f32[8,128,512]{2,1,0:T(8,128)} fusion(bf16[8,2,256,128]{2,3,0,1:T(8,128)(2,1)S(1)} %copy.35, bf16[2,512,256]{2,1,0:T(8,128)(2,1)S(1)} %copy-done), kind=kOutput, calls=%fused_computation.54 | convolution fusion | flops 268435456 | bytes 2883584 | tf_op jit(solution)/shard_map/ku,bua->bka/dot_general | solution.py:89
  3.4 0.0 copy-done.1
  3.4 0.0 copy-start.7
  3.4 0.5 fusion.49
  3.9 0.2 copy-done.7
  4.1 0.1 constant_dynamic-slice_fusion
  4.2 0.0 copy-start.2
  4.2 2.2 %convolution_add_fusion = f32[8,128,512]{2,1,0:T(8,128)S(1)} fusion(f32[8,128,512]{2,1,0:T(8,128)} %fusion.50, bf16[8,2,256,128]{2,3,0,1:T(8,128)(2,1)S(1)} %copy.35, bf16[2,512,256]{2,1,0:T(8,128)(2,1)} %param.9), kind=kOutput, calls=%fused_computation.21 | convolution fusion | flops 268959744 | bytes 4980736 | tf_op jit(solution)/shard_map/ku,bua->bka/dot_general | solution.py:89
  6.4 0.1 fusion.89
  6.6 0.0 copy-done.2
  6.6 0.8 fusion.39
  7.4 0.2 pad_maximum_fusion.1
  7.6 3.1 %copy.44 = bf16[1,8,512,2,128]{4,1,3,0,2:T(8,128)(2,1)} copy(bf16[1,8,512,2,128]{2,4,1,3,0:T(8,128)(2,1)S(1)} %pad_maximum_fusion.1) | data formatting | bytes 4194304 | tf_op jit(solution)/shard_map/stack | solution.py:96
  10.7 0.0 copy-start.8
  10.7 6.2 %all-to-all-start = ((bf16[1,8,512,2,128]{4,1,3,0,2:T(8,128)(2,1)}), bf16[1,8,512,2,128]{4,1,3,0,2:T(8,128)(2,1)S(1)}, u32[]{:S(2)}, u32[]{:S(2)}) async-start(bf16[1,8,512,2,128]{4,1,3,0,2:T(8,128)(2,1)} %copy.44), calls=%async_computation | async-start | bytes 4194304 | tf_op jit(solution)/shard_map/all_to_all | solution.py:99
  17.0 0.0 copy-done.8
  17.0 0.1 fusion.91
  17.2 44.8 %all-to-all-done = bf16[1,8,512,2,128]{4,1,3,0,2:T(8,128)(2,1)S(1)} async-done(((bf16[1,8,512,2,128]{4,1,3,0,2:T(8,128)(2,1)}), bf16[1,8,512,2,128]{4,1,3,0,2:T(8,128)(2,1)S(1)}, u32[]{:S(2)}, u32[]{:S(2)}) %all-to-all-start) | async-done | bytes 2097184 | tf_op jit(solution)/shard_map/all_to_all | solution.py:99
  62.0 0.5 copy.45
  62.5 3.2 %copy.46 = bf16[32,1,8,16,2,128]{5,4,3,2,0,1:T(2,128)(2,1)S(1)} copy(bf16[32,1,8,16,2,128]{5,3,0,4,2,1:T(8,128)(2,1)S(1)} %bitcast.191) | data formatting | bytes 4194304 | tf_op jit(solution)/shard_map/all_to_all | solution.py:99
  65.7 2.8 %reshape.499 = bf16[256,4096]{1,0:T(8,128)(2,1)} reshape(bf16[32,1,8,16,2,128]{5,4,3,2,0,1:T(2,128)(2,1)S(1)} %copy.46) | data formatting | bytes 4194304 | tf_op jit(solution)/shard_map/reshape | solution.py:100
  68.6 3.3 %copy.47 = bf16[4096,256]{1,0:T(8,128)(2,1)S(1)} copy(bf16[4096,256]{0,1:T(8,128)(2,1)} %bitcast.192) | data formatting | bytes 4194304 | tf_op jit(solution)/shard_map/dot_general | solution.py:102
  71.8 1.8 %fusion.72 = f32[256,16,2,128]{3,0,2,1:T(8,128)S(1)} fusion(bf16[16,2,128,256]{3,2,1,0:T(8,128)(2,1)S(1)} %bitcast.193, f32[256]{0:T(256)S(1)} %bitcast.199, f32[256]{0:T(256)S(1)} %bitcast.197, f32[256]{0:T(256)S(1)} %bitcast.195, s32[256]{0:T(256)S(1)} %get-tuple-element.29, s32[256]{0:T(256)S(1)} %get-tuple-element.30, ...), kind=kOutput, calls=%fused_computation.80 | convolution fusion | flops 538312704 | bytes 6297088 | tf_op jit(solution)/shard_map/dot_general | solution.py:102
  73.6 1.4 fusion.41
  75.1 1.2 copy.48
  76.3 1.2 copy.49
  77.5 1.5 pad_maximum_fusion.2
  79.0 7.8 %all-to-all-start.1 = ((bf16[32,8,16,2,128]{4,2,3,1,0:T(8,128)(2,1)}), bf16[32,8,16,2,128]{4,2,3,1,0:T(8,128)(2,1)S(1)}, u32[]{:S(2)}, u32[]{:S(2)}) async-start(bf16[32,8,16,2,128]{4,2,3,1,0:T(8,128)(2,1)} %pad_maximum_fusion.2), calls=%async_computation.1 | async-start | bytes 4194304 | tf_op jit(solution)/shard_map/all_to_all | solution.py:114
  86.9 3.1 %collective-permute-start = (bf16[1,2,256,128]{2,3,0,1:T(8,128)(2,1)S(1)}, bf16[1,2,256,128]{2,3,0,1:T(8,128)(2,1)S(1)}, u32[]{:S(2)}, u32[]{:S(2)}) collective-permute-start(bf16[1,2,256,128]{2,3,0,1:T(8,128)(2,1)S(1)} %get-tuple-element.13), channel_id=1, source_target_pairs={{0,1},{1,2},{2,3},{3,4},{4,5},{5,6},{6,7},{7,8},{8,9},{9,10},{10,1... | collective-permute-start | bytes 393224 | tf_op jit(solution)/shard_map/ppermute | solution.py:17
  90.0 3.3 %collective-permute-start.1 = (bf16[1,2,256,128]{2,3,0,1:T(8,128)(2,1)S(1)}, bf16[1,2,256,128]{2,3,0,1:T(8,128)(2,1)S(1)}, u32[]{:S(2)}, u32[]{:S(2)}) collective-permute-start(bf16[1,2,256,128]{2,3,0,1:T(8,128)(2,1)S(1)} %get-tuple-element.14), channel_id=1, source_target_pairs={{1,0},{2,1},{3,2},{4,3},{5,4},{6,5},{7,6},{8,7},{9,8},{10,9},{11,1... | collective-permute-start | bytes 393224 | tf_op jit(solution)/shard_map/ppermute | solution.py:20
  93.3 0.1 dynamic-slice_convert_fusion
  93.4 44.3 %collective-permute-done = bf16[1,2,256,128]{2,3,0,1:T(8,128)(2,1)S(1)} collective-permute-done((bf16[1,2,256,128]{2,3,0,1:T(8,128)(2,1)S(1)}, bf16[1,2,256,128]{2,3,0,1:T(8,128)(2,1)S(1)}, u32[]{:S(2)}, u32[]{:S(2)}) %collective-permute-start) | collective-permute-done | bytes 131104 | tf_op jit(solution)/shard_map/ppermute | solution.py:17
  137.7 0.0 collective-permute-done.1
  137.7 0.0 slice-start
  137.7 0.2 fusion.46
  137.9 0.0 slice-start.1
  137.9 0.3 pad_maximum_fusion
  138.2 3.3 %fusion.13 = f32[8,128,256]{2,1,0:T(8,128)S(1)} fusion(bf16[8,3,2,256,256]{4,3,2,1,0:T(8,128)(2,1)} %param.7, bf16[8,3,2,256,128]{3,4,1,0,2:T(8,128)(2,1)S(1)} %pad_maximum_fusion), kind=kOutput, calls=%fused_computation.25 | convolution fusion | flops 402653184 | bytes 5767168 | tf_op jit(solution)/shard_map/bjuv,bjva->bua/dot_general | solution.py:67
  141.6 0.0 slice-done
  141.6 0.0 slice-done.1
  141.6 1.1 fusion.16
  142.7 2.1 %fusion.36 = f32[8,1,256,128]{2,3,0,1:T(8,128)} fusion(f32[8,128,256]{2,1,0:T(8,128)S(1)} %fusion.13, bf16[8,3,2,256,256]{4,3,2,1,0:T(8,128)(2,1)S(1)} %bitcast.201, bf16[8,3,2,256,128]{3,4,1,0,2:T(8,128)(2,1)S(1)} %pad_maximum_fusion), kind=kOutput, calls=%fused_computation.36 | convolution fusion | flops 402915328 | bytes 6815744 | tf_op jit(solution)/shard_map/bjuv,bjva->bua/dot_general | solution.py:67
  144.8 2.1 %fusion.30 = f32[8,1,256,128]{2,3,0,1:T(8,128)} fusion(f32[8,128,256]{2,1,0:T(8,128)S(1)} %fusion.16, bf16[8,3,2,256,256]{4,3,2,1,0:T(8,128)(2,1)S(1)} %bitcast.201, bf16[8,3,2,256,128]{3,4,1,0,2:T(8,128)(2,1)S(1)} %pad_maximum_fusion), kind=kOutput, calls=%fused_computation.34 | convolution fusion | flops 402915328 | bytes 6815744 | tf_op jit(solution)/shard_map/bjuv,bjva->bua/dot_general | solution.py:67
  147.0 0.0 copy-start.3
  147.0 0.0 all-to-all-done.1
  147.0 0.5 copy.50
  147.5 0.5 copy-done.3
  148.0 0.0 copy-start.4
  148.0 0.5 fusion.47
  148.5 0.5 fusion.48
  149.0 0.1 copy-done.4
  149.1 0.5 fusion.26
  149.5 0.0 copy-start.5
  149.6 0.0 copy-start.6
  149.6 0.5 fusion.25
  150.1 0.7 copy-done.5
  150.8 0.3 copy-done.6
  151.1 0.5 fusion.12
  151.6 1.3 copy.53
  (11 shorter events, 0.2 us)
Async XLA Ops:
  0.0 1.6 %copy-start = (bf16[2,512,256]{2,1,0:T(8,128)(2,1)S(1)}, bf16[2,512,256]{2,1,0:T(8,128)(2,1)}, u32[]{:S(2)}) copy-start(bf16[2,512,256]{2,1,0:T(8,128)(2,1)} %param.9) | copy-start | bytes 1572868
  1.6 1.8 %copy-start.1 = (bf16[2,512,256]{2,1,0:T(8,128)(2,1)S(1)}, bf16[2,512,256]{2,1,0:T(8,128)(2,1)}, u32[]{:S(2)}) copy-start(bf16[2,512,256]{2,1,0:T(8,128)(2,1)} %param.9) | copy-start | bytes 1572868
  3.4 0.7 copy-start.7
  4.2 2.4 %copy-start.2 = (bf16[2,512,256]{2,1,0:T(8,128)(2,1)S(1)}, bf16[2,512,256]{2,1,0:T(8,128)(2,1)}, u32[]{:S(2)}) copy-start(bf16[2,512,256]{2,1,0:T(8,128)(2,1)} %param.9) | copy-start | bytes 1572868
  10.7 6.3 %copy-start.8 = (s32[2,256]{1,0:T(2,128)S(1)}, s32[2,256]{1,0:T(2,128)}, u32[]{:S(2)}) copy-start(s32[2,256]{1,0:T(2,128)} %param.8) | copy-start | bytes 6148
  10.7 51.3 %all-to-all-start = ((bf16[1,8,512,2,128]{4,1,3,0,2:T(8,128)(2,1)}), bf16[1,8,512,2,128]{4,1,3,0,2:T(8,128)(2,1)S(1)}, u32[]{:S(2)}, u32[]{:S(2)}) async-start(bf16[1,8,512,2,128]{4,1,3,0,2:T(8,128)(2,1)} %copy.44), calls=%async_computation | async-start | bytes 4194304 | tf_op jit(solution)/shard_map/all_to_all | solution.py:99
  79.0 68.0 %all-to-all-start.1 = ((bf16[32,8,16,2,128]{4,2,3,1,0:T(8,128)(2,1)}), bf16[32,8,16,2,128]{4,2,3,1,0:T(8,128)(2,1)S(1)}, u32[]{:S(2)}, u32[]{:S(2)}) async-start(bf16[32,8,16,2,128]{4,2,3,1,0:T(8,128)(2,1)} %pad_maximum_fusion.2), calls=%async_computation.1 | async-start | bytes 4194304 | tf_op jit(solution)/shard_map/all_to_all | solution.py:114
  86.9 50.8 %collective-permute-start = (bf16[1,2,256,128]{2,3,0,1:T(8,128)(2,1)S(1)}, bf16[1,2,256,128]{2,3,0,1:T(8,128)(2,1)S(1)}, u32[]{:S(2)}, u32[]{:S(2)}) collective-permute-start(bf16[1,2,256,128]{2,3,0,1:T(8,128)(2,1)S(1)} %get-tuple-element.13), channel_id=1, source_target_pairs={{0,1},{1,2},{2,3},{3,4},{4,5},{5,6},{6,7},{7,8},{8,9},{9,10},{10,1... | collective-permute-start | bytes 393224 | tf_op jit(solution)/shard_map/ppermute | solution.py:17
  90.0 47.7 %collective-permute-start.1 = (bf16[1,2,256,128]{2,3,0,1:T(8,128)(2,1)S(1)}, bf16[1,2,256,128]{2,3,0,1:T(8,128)(2,1)S(1)}, u32[]{:S(2)}, u32[]{:S(2)}) collective-permute-start(bf16[1,2,256,128]{2,3,0,1:T(8,128)(2,1)S(1)} %get-tuple-element.14), channel_id=1, source_target_pairs={{1,0},{2,1},{3,2},{4,3},{5,4},{6,5},{7,6},{8,7},{9,8},{10,9},{11,1... | collective-permute-start | bytes 393224 | tf_op jit(solution)/shard_map/ppermute | solution.py:20
  137.7 3.9 %slice-start = ((s8[6291456]{0:T(1024)(128)(4,1)}), s8[4194304]{0:T(1024)(128)(4,1)S(1)}, s32[]{:S(2)}) async-start(s8[6291456]{0:T(1024)(128)(4,1)} %bitcast.200), calls=%async_computation.2 | async-start | bytes 8388608
  137.9 3.7 %slice-start.1 = ((s8[6291456]{0:T(1024)(128)(4,1)}), s8[2097152]{0:T(1024)(128)(4,1)S(1)}, s32[]{:S(2)}) async-start(s8[6291456]{0:T(1024)(128)(4,1)} %bitcast.200), calls=%async_computation.3 | async-start | bytes 4194304
  147.0 1.0 copy-start.3
  148.0 1.0 copy-start.4
  149.5 1.2 copy-start.5
  149.6 1.5 %copy-start.6 = (f32[8,1,256,128]{2,3,0,1:T(8,128)S(1)}, f32[8,1,256,128]{2,3,0,1:T(8,128)}, u32[]{:S(2)}) copy-start(f32[8,1,256,128]{2,3,0,1:T(8,128)} %fusion.30) | copy-start | bytes 3145732
where the time goes:
time: 153 us
  waiting for transfers between devices  89.1 us (58%)
  local copies, waits for them, and re-layouts  20.7 us (14%)
  starting transfers between devices  20.5 us (13%)
  matrix products  17.7 us (12%)
  other arithmetic  4.68 us (3%)
    all_to_all x1, waiting for transfers between devices, local(): lax.all_to_all(pattern[None], ('box', 'dir'), split_axis=2, concat_axis=0...  44.8 us
    ppermute x1, waiting for transfers between devices, extended(): lax.ppermute(lax.slice_in_dim(block, block.shape[dim] - width, None, axis...  44.3 us
    dot_general x4, matrix products, product(): jnp.einsum('bjuv,bjva->bua', left, right, preferred_element_type=jnp.floa...  8.69 us
    all_to_all x1, starting transfers between devices, local(): lax.all_to_all(shaped_back, ('box', 'dir'), split_axis=0, concat_axis=2,...  7.83 us
    all_to_all x1, starting transfers between devices, local(): lax.all_to_all(pattern[None], ('box', 'dir'), split_axis=2, concat_axis=0...  6.23 us
    dot_general x4, matrix products, gather_in(): jnp.einsum('ku,bua->bka', matrix, vectors, preferred_element_type=jnp.flo...  5.26 us
    all_to_all x2, local copies, waits for them, and re-layouts, local(): lax.all_to_all(pattern[None], ('box', 'dir'), split_axis=2, concat_axis=0...  3.78 us
    unnamed x23, local copies, waits for them, and re-layouts  3.38 us
  transfers between devices with their start and end apart: 4, of which 2 were waited for; matrix products, arithmetic and copies ran while one was open for 6% of the time, Pallas kernels for 0%

commit v1 on v0

--- a/solution.py
+++ b/solution.py
@@ -111,7 +111,15 @@
         [cos_all * sum_re - sin_all * sum_im, cos_all * sum_im + sin_all * sum_re], 2
     ).astype(jnp.bfloat16)
     shaped_back = received.reshape(devices, box_count, dir_share, 2, angle_count)
-    returned = lax.all_to_all(shaped_back, ("box", "dir"), split_axis=0, concat_axis=2, tiled=True)
+    returned = jnp.concatenate(
+        lax.all_to_all(
+            jnp.stack(jnp.split(shaped_back, lax.axis_size(("box", "dir")), axis=0)),
+            ("box", "dir"),
+            0,
+            0,
+        ),
+        axis=2,
+    )
     returned = returned.reshape(box_count, dir_count, 2, angle_count)
 
     def spread_out(matrix, vectors):

time: 153 us -> 174 us (1.14)
  other arithmetic: 4.68 us -> 23.4 us
    unnamed x1 -> x32, other arithmetic: 0.01 us -> 19.7 us
    another operation x2 -> x0, local copies, waits for them, and re-layouts: 2.44 us -> none  [local(): jnp.stack([cos_all * sum_re - sin_all * sum_im, cos_all * sum_im + sin_al...]
    unnamed x23 -> x25, local copies, waits for them, and re-layouts: 3.38 us -> 5.25 us
where the time goes in v1:
time: 174 us; the launch traced here: 173 us
  waiting for transfers between devices  89.1 us (51%)
  other arithmetic  23.4 us (13%)
  local copies, waits for them, and re-layouts  21.1 us (12%)
  starting transfers between devices  20.4 us (12%)
  matrix products  18.6 us (11%)
    all_to_all x1, waiting for transfers between devices, local(): lax.all_to_all(pattern[None], ('box', 'dir'), split_axis=2, concat_axis=0...  44.8 us
    ppermute x1, waiting for transfers between devices, extended(): lax.ppermute(lax.slice_in_dim(block, block.shape[dim] - width, None, axis...  44.3 us
    unnamed x32, other arithmetic  19.7 us
    dot_general x4, matrix products, product(): jnp.einsum('bjuv,bjva->bua', left, right, preferred_element_type=jnp.floa...  8.7 us
    all_to_all x1, starting transfers between devices, local(): lax.all_to_all(jnp.stack(jnp.split(shaped_back, lax.axis_size(('box', 'di...  7.83 us
    all_to_all x1, starting transfers between devices, local(): lax.all_to_all(pattern[None], ('box', 'dir'), split_axis=2, concat_axis=0...  6.23 us
    dot_general x4, matrix products, gather_in(): jnp.einsum('ku,bua->bka', matrix, vectors, preferred_element_type=jnp.flo...  5.26 us
    unnamed x25, local copies, waits for them, and re-layouts  5.25 us
  transfers between devices with their start and end apart: 4, of which 2 were waited for; matrix products, arithmetic and copies ran while one was open for 6% of the time, Pallas kernels for 0%

profile of v1, /device:TPU:17, one launch (start us, length us, event | category | flops | bytes accessed | tf_op | source)
XLA Modules:
  0.0 173.0 jit_solution(6356707030455421786)
XLA Ops:
  0.1 1.5 copy.34
  1.6 1.8 %fusion.52 = f32[8,128,512]{2,1,0:T(8,128)} fusion(bf16[8,2,256,128]{2,3,0,1:T(8,128)(2,1)S(1)} %copy.34, bf16[2,512,256]{2,1,0:T(8,128)(2,1)S(1)} %copy-done.1), kind=kOutput, calls=%fused_computation.115 | convolution fusion | flops 268435456 | bytes 2883584 | tf_op jit(solution)/shard_map/ku,bua->bka/dot_general | solution.py:89
  3.4 0.5 fusion.51
  4.2 2.2 %convolution_add_fusion = f32[8,128,512]{2,1,0:T(8,128)S(1)} fusion(f32[8,128,512]{2,1,0:T(8,128)} %fusion.52, bf16[8,2,256,128]{2,3,0,1:T(8,128)(2,1)S(1)} %copy.34, bf16[2,512,256]{2,1,0:T(8,128)(2,1)} %param.9), kind=kOutput, calls=%fused_computation.82 | convolution fusion | flops 268959744 | bytes 4980736 | tf_op jit(solution)/shard_map/ku,bua->bka/dot_general | solution.py:89
  6.6 0.8 fusion.39
  7.6 3.1 %copy.43 = bf16[1,8,512,2,128]{4,1,3,0,2:T(8,128)(2,1)} copy(bf16[1,8,512,2,128]{2,4,1,3,0:T(8,128)(2,1)S(1)} %pad_maximum_fusion.1) | data formatting | bytes 4194304 | tf_op jit(solution)/shard_map/stack | solution.py:96
  10.7 6.2 %all-to-all-start = ((bf16[1,8,512,2,128]{4,1,3,0,2:T(8,128)(2,1)}), bf16[1,8,512,2,128]{4,1,3,0,2:T(8,128)(2,1)S(1)}, u32[]{:S(2)}, u32[]{:S(2)}) async-start(bf16[1,8,512,2,128]{4,1,3,0,2:T(8,128)(2,1)} %copy.43), calls=%async_computation | async-start | bytes 4194304 | tf_op jit(solution)/shard_map/all_to_all | solution.py:99
  17.2 44.8 %all-to-all-done = bf16[1,8,512,2,128]{4,1,3,0,2:T(8,128)(2,1)S(1)} async-done(((bf16[1,8,512,2,128]{4,1,3,0,2:T(8,128)(2,1)}), bf16[1,8,512,2,128]{4,1,3,0,2:T(8,128)(2,1)S(1)}, u32[]{:S(2)}, u32[]{:S(2)}) %all-to-all-start) | async-done | bytes 2097184 | tf_op jit(solution)/shard_map/all_to_all | solution.py:99
  62.0 0.5 copy.44
  62.5 3.2 %copy.45 = bf16[32,1,8,16,2,128]{5,4,3,2,0,1:T(2,128)(2,1)S(1)} copy(bf16[32,1,8,16,2,128]{5,3,0,4,2,1:T(8,128)(2,1)S(1)} %bitcast.246) | data formatting | bytes 4194304 | tf_op jit(solution)/shard_map/all_to_all | solution.py:99
  65.8 2.8 %reshape.558 = bf16[256,4096]{1,0:T(8,128)(2,1)} reshape(bf16[32,1,8,16,2,128]{5,4,3,2,0,1:T(2,128)(2,1)S(1)} %copy.45) | data formatting | bytes 4194304 | tf_op jit(solution)/shard_map/reshape | solution.py:100
  68.6 3.3 %copy.46 = bf16[4096,256]{1,0:T(8,128)(2,1)S(1)} copy(bf16[4096,256]{0,1:T(8,128)(2,1)} %bitcast.247) | data formatting | bytes 4194304 | tf_op jit(solution)/shard_map/dot_general | solution.py:102
  71.8 1.8 %fusion.74 = f32[256,16,2,128]{3,0,2,1:T(8,128)S(1)} fusion(bf16[16,2,128,256]{3,2,1,0:T(8,128)(2,1)S(1)} %bitcast.248, f32[256]{0:T(256)S(1)} %bitcast.254, f32[256]{0:T(256)S(1)} %bitcast.252, f32[256]{0:T(256)S(1)} %bitcast.250, s32[256]{0:T(256)S(1)} %get-tuple-element.31, s32[256]{0:T(256)S(1)} %get-tuple-element.32, ...), kind=kOutput, calls=%fused_computation.141 | convolution fusion | flops 538312704 | bytes 6297088 | tf_op jit(solution)/shard_map/dot_general | solution.py:102
  73.6 1.4 subtract_convert_fusion
  75.1 0.6 constant_dynamic-update-slice_fusion.31
  75.7 0.6 constant_dynamic-update-slice_fusion.30
  76.3 0.6 constant_dynamic-update-slice_fusion.29
  77.0 0.6 constant_dynamic-update-slice_fusion.28
  77.6 0.6 constant_dynamic-update-slice_fusion.27
  78.2 0.6 constant_dynamic-update-slice_fusion.26
  78.9 0.6 constant_dynamic-update-slice_fusion.25
  79.5 0.6 constant_dynamic-update-slice_fusion.24
  80.2 0.7 constant_dynamic-update-slice_fusion.23
  80.8 0.6 constant_dynamic-update-slice_fusion.22
  81.4 0.6 constant_dynamic-update-slice_fusion.21
  82.1 0.6 constant_dynamic-update-slice_fusion.20
  82.7 0.6 constant_dynamic-update-slice_fusion.19
  83.3 0.6 constant_dynamic-update-slice_fusion.18
  84.0 0.6 constant_dynamic-update-slice_fusion.17
  84.6 0.6 constant_dynamic-update-slice_fusion.16
  85.2 0.6 constant_dynamic-update-slice_fusion.15
  85.9 0.6 constant_dynamic-update-slice_fusion.14
  86.5 0.6 constant_dynamic-update-slice_fusion.13
  87.2 0.6 constant_dynamic-update-slice_fusion.12
  87.8 0.6 constant_dynamic-update-slice_fusion.11
  88.4 0.6 constant_dynamic-update-slice_fusion.10
  89.1 0.6 constant_dynamic-update-slice_fusion.9
  89.7 0.6 constant_dynamic-update-slice_fusion.8
  90.3 0.6 constant_dynamic-update-slice_fusion.7
  91.0 0.6 constant_dynamic-update-slice_fusion.6
  91.6 0.6 constant_dynamic-update-slice_fusion.5
  92.2 0.6 constant_dynamic-update-slice_fusion.4
  92.9 0.6 constant_dynamic-update-slice_fusion.3
  93.5 0.6 constant_dynamic-update-slice_fusion.2
  94.1 0.6 constant_dynamic-update-slice_fusion.1
  94.8 0.6 constant_dynamic-update-slice_fusion
  95.4 7.8 %all-to-all-start.1 = ((bf16[32,1,8,16,2,128]{5,2,4,3,1,0:T(8,128)(2,1)}), bf16[32,1,8,16,2,128]{5,2,4,3,1,0:T(8,128)(2,1)S(1)}, u32[]{:S(2)}, u32[]{:S(2)}) async-start(bf16[32,1,8,16,2,128]{5,2,4,3,1,0:T(8,128)(2,1)} %constant_dynamic-update-slice_fusion), calls=%async_computation.1 | async-start | bytes 4194304 | tf_op jit(solution)/shard_map/all_to_all | solution.py:115
  103.3 3.1 %collective-permute-start = (bf16[1,2,256,128]{2,3,0,1:T(8,128)(2,1)S(1)}, bf16[1,2,256,128]{2,3,0,1:T(8,128)(2,1)S(1)}, u32[]{:S(2)}, u32[]{:S(2)}) collective-permute-start(bf16[1,2,256,128]{2,3,0,1:T(8,128)(2,1)S(1)} %get-tuple-element.15), channel_id=1, source_target_pairs={{0,1},{1,2},{2,3},{3,4},{4,5},{5,6},{6,7},{7,8},{8,9},{9,10},{10,1... | collective-permute-start | bytes 393224 | tf_op jit(solution)/shard_map/ppermute | solution.py:17
  106.4 3.3 %collective-permute-start.1 = (bf16[1,2,256,128]{2,3,0,1:T(8,128)(2,1)S(1)}, bf16[1,2,256,128]{2,3,0,1:T(8,128)(2,1)S(1)}, u32[]{:S(2)}, u32[]{:S(2)}) collective-permute-start(bf16[1,2,256,128]{2,3,0,1:T(8,128)(2,1)S(1)} %get-tuple-element.16), channel_id=1, source_target_pairs={{1,0},{2,1},{3,2},{4,3},{5,4},{6,5},{7,6},{8,7},{9,8},{10,9},{11,1... | collective-permute-start | bytes 393224 | tf_op jit(solution)/shard_map/ppermute | solution.py:20
  109.7 44.3 %collective-permute-done = bf16[1,2,256,128]{2,3,0,1:T(8,128)(2,1)S(1)} collective-permute-done((bf16[1,2,256,128]{2,3,0,1:T(8,128)(2,1)S(1)}, bf16[1,2,256,128]{2,3,0,1:T(8,128)(2,1)S(1)}, u32[]{:S(2)}, u32[]{:S(2)}) %collective-permute-start) | collective-permute-done | bytes 131104 | tf_op jit(solution)/shard_map/ppermute | solution.py:17
  154.6 3.3 %fusion.13 = f32[8,128,256]{2,1,0:T(8,128)S(1)} fusion(bf16[8,3,2,256,256]{4,3,2,1,0:T(8,128)(2,1)} %param.7, bf16[8,3,2,256,128]{3,4,1,0,2:T(8,128)(2,1)S(1)} %pad_maximum_fusion), kind=kOutput, calls=%fused_computation.86 | convolution fusion | flops 402653184 | bytes 5767168 | tf_op jit(solution)/shard_map/bjuv,bjva->bua/dot_general | solution.py:67
  158.0 1.1 fusion.16
  159.1 2.1 %fusion.36 = f32[8,1,256,128]{2,3,0,1:T(8,128)} fusion(f32[8,128,256]{2,1,0:T(8,128)S(1)} %fusion.13, bf16[8,3,2,256,256]{4,3,2,1,0:T(8,128)(2,1)S(1)} %bitcast.256, bf16[8,3,2,256,128]{3,4,1,0,2:T(8,128)(2,1)S(1)} %pad_maximum_fusion), kind=kOutput, calls=%fused_computation.97 | convolution fusion | flops 402915328 | bytes 6815744 | tf_op jit(solution)/shard_map/bjuv,bjva->bua/dot_general | solution.py:67
  161.2 2.1 %fusion.30 = f32[8,1,256,128]{2,3,0,1:T(8,128)} fusion(f32[8,128,256]{2,1,0:T(8,128)S(1)} %fusion.16, bf16[8,3,2,256,256]{4,3,2,1,0:T(8,128)(2,1)S(1)} %bitcast.256, bf16[8,3,2,256,128]{3,4,1,0,2:T(8,128)(2,1)S(1)} %pad_maximum_fusion), kind=kOutput, calls=%fused_computation.95 | convolution fusion | flops 402915328 | bytes 6815744 | tf_op jit(solution)/shard_map/bjuv,bjva->bua/dot_general | solution.py:67
  163.4 1.5 fusion.130
  164.8 1.7 copy.57
  166.6 0.7 copy.58
  167.3 1.5 fusion.49
  168.8 0.5 fusion.45
  169.2 0.5 fusion.26
  169.7 0.5 fusion.25
  170.2 0.7 copy-done.5
  171.2 0.5 fusion.12
  171.7 1.3 copy.49
  (41 shorter events, 1.9 us)
Async XLA Ops:
  0.0 1.6 copy-start.1
  1.6 1.8 %copy-start.2 = (bf16[2,512,256]{2,1,0:T(8,128)(2,1)S(1)}, bf16[2,512,256]{2,1,0:T(8,128)(2,1)}, u32[]{:S(2)}) copy-start(bf16[2,512,256]{2,1,0:T(8,128)(2,1)} %param.9) | copy-start | bytes 1572868
  3.4 0.7 copy-start.7
  4.2 2.4 %copy-start.3 = (bf16[2,512,256]{2,1,0:T(8,128)(2,1)S(1)}, bf16[2,512,256]{2,1,0:T(8,128)(2,1)}, u32[]{:S(2)}) copy-start(bf16[2,512,256]{2,1,0:T(8,128)(2,1)} %param.9) | copy-start | bytes 1572868
  10.7 6.3 %copy-start.8 = (s32[2,256]{1,0:T(2,128)S(1)}, s32[2,256]{1,0:T(2,128)}, u32[]{:S(2)}) copy-start(s32[2,256]{1,0:T(2,128)} %param.8) | copy-start | bytes 6148
  10.7 51.3 %all-to-all-start = ((bf16[1,8,512,2,128]{4,1,3,0,2:T(8,128)(2,1)}), bf16[1,8,512,2,128]{4,1,3,0,2:T(8,128)(2,1)S(1)}, u32[]{:S(2)}, u32[]{:S(2)}) async-start(bf16[1,8,512,2,128]{4,1,3,0,2:T(8,128)(2,1)} %copy.43), calls=%async_computation | async-start | bytes 4194304 | tf_op jit(solution)/shard_map/all_to_all | solution.py:99
  95.4 68.0 %all-to-all-start.1 = ((bf16[32,1,8,16,2,128]{5,2,4,3,1,0:T(8,128)(2,1)}), bf16[32,1,8,16,2,128]{5,2,4,3,1,0:T(8,128)(2,1)S(1)}, u32[]{:S(2)}, u32[]{:S(2)}) async-start(bf16[32,1,8,16,2,128]{5,2,4,3,1,0:T(8,128)(2,1)} %constant_dynamic-update-slice_fusion), calls=%async_computation.1 | async-start | bytes 4194304 | tf_op jit(solution)/shard_map/all_to_all | solution.py:115
  103.3 50.8 %collective-permute-start = (bf16[1,2,256,128]{2,3,0,1:T(8,128)(2,1)S(1)}, bf16[1,2,256,128]{2,3,0,1:T(8,128)(2,1)S(1)}, u32[]{:S(2)}, u32[]{:S(2)}) collective-permute-start(bf16[1,2,256,128]{2,3,0,1:T(8,128)(2,1)S(1)} %get-tuple-element.15), channel_id=1, source_target_pairs={{0,1},{1,2},{2,3},{3,4},{4,5},{5,6},{6,7},{7,8},{8,9},{9,10},{10,1... | collective-permute-start | bytes 393224 | tf_op jit(solution)/shard_map/ppermute | solution.py:17
  106.4 47.7 %collective-permute-start.1 = (bf16[1,2,256,128]{2,3,0,1:T(8,128)(2,1)S(1)}, bf16[1,2,256,128]{2,3,0,1:T(8,128)(2,1)S(1)}, u32[]{:S(2)}, u32[]{:S(2)}) collective-permute-start(bf16[1,2,256,128]{2,3,0,1:T(8,128)(2,1)S(1)} %get-tuple-element.16), channel_id=1, source_target_pairs={{1,0},{2,1},{3,2},{4,3},{5,4},{6,5},{7,6},{8,7},{9,8},{10,9},{11,1... | collective-permute-start | bytes 393224 | tf_op jit(solution)/shard_map/ppermute | solution.py:20
  154.0 3.9 %slice-start = ((s8[6291456]{0:T(1024)(128)(4,1)}), s8[4194304]{0:T(1024)(128)(4,1)S(1)}, s32[]{:S(2)}) async-start(s8[6291456]{0:T(1024)(128)(4,1)} %bitcast.255), calls=%async_computation.2 | async-start | bytes 8388608
  154.3 3.7 %slice-start.1 = ((s8[6291456]{0:T(1024)(128)(4,1)}), s8[2097152]{0:T(1024)(128)(4,1)S(1)}, s32[]{:S(2)}) async-start(s8[6291456]{0:T(1024)(128)(4,1)} %bitcast.255), calls=%async_computation.3 | async-start | bytes 4194304
  164.8 1.7 copy-start
  167.3 1.5 copy-start.4
  169.7 1.2 copy-start.5
  169.7 1.5 copy-start.6
